TPU v7x, 32 devices: a whole 2x2x4 slice. The times are simulated.
32 devices in a mesh: fsdp: 8 (over z, x), ctx: 4 (over y, core).
Axes of the slice: x: 2, y: 2, z: 4, core: 2. Of those that a mesh axis runs over, the one named last changes fastest.
Arguments:
- inputs: bfloat16 [4096, 768], P(('fsdp', 'ctx')), may hold values from -6 to 6
- lengths: int32 [8, 3], P('fsdp'), may hold values from 1 to 384, 512 in all within a row
- norm1_gain: bfloat16 [768], P(('fsdp', 'ctx')), may hold values from 0.5 to 1.5
- qkv_weight: bfloat16 [768, 2304], P(('fsdp', 'ctx'))
- attn_out_weight: bfloat16 [768, 768], P(('fsdp', 'ctx')), may hold values from -2.5 to 2.5
- norm2_gain: bfloat16 [768], P(('fsdp', 'ctx')), may hold values from 0.5 to 1.5
- ffn_in_weight: bfloat16 [768, 2304], P(('fsdp', 'ctx')), may hold values from -0.21875 to 0.21875
- ffn_out_weight: bfloat16 [1152, 768], P(None, ('fsdp', 'ctx')), may hold values from -0.1875 to 0.1875
- out_grad: bfloat16 [4096, 768], P(('fsdp', 'ctx')), may hold values from -6 to 6
Outputs:
- outputs: bfloat16 [4096, 768], P(('fsdp', 'ctx'))
- input_grad: bfloat16 [4096, 768], P(('fsdp', 'ctx'))
- norm1_gain_grad: float32 [768], P(('fsdp', 'ctx'))
- qkv_weight_grad: float32 [768, 2304], P(('fsdp', 'ctx'))
- attn_out_weight_grad: float32 [768, 768], P(('fsdp', 'ctx'))
- norm2_gain_grad: float32 [768], P(('fsdp', 'ctx'))
- ffn_in_weight_grad: float32 [768, 2304], P(('fsdp', 'ctx'))
- ffn_out_weight_grad: float32 [1152, 768], P(None, ('fsdp', 'ctx'))
Inputs may be any that keep to these rules, and one draw needn't show every extreme that they name: `lengths`: each row sums to 512, and its largest entry is exactly 384.
All inputs are finite; a program needn't handle non-finite values.
Results may differ from a plain program's by a relative error of at most 0.038.
The roundings to bfloat16 on the way count: a program that leaves them out, or rounds other values in their place, can miss the bound.
Values may be sent and summed in bfloat16 or wider, within the bound.
No kernel may reach another device: no remote copies, remote signals or barrier semaphores. Data moves between devices by JAX's collectives and lax.ppermute only.
A program may use at most 128 MiB of HBM per device.

v0:
```python
import math
import jax
import jax.numpy as jnp
from jax import lax
from jax.sharding import PartitionSpec as P

rope_base = 160000.0
norm_eps = 1e-05
score_scale = 0.125


def positions(length_row, index_rows):
    seq_ends = jnp.cumsum(length_row)
    starts = seq_ends - length_row
    segment = jnp.sum((index_rows[:, None] >= seq_ends[None, :]).astype(jnp.int32), axis=1)
    seq_numbers = jnp.arange(length_row.shape[0], dtype=jnp.int32)
    seq_start = jnp.sum(
        jnp.where(segment[:, None] == seq_numbers[None, :], starts[None, :], 0), axis=1
    )
    return (segment, index_rows - seq_start)


def rope_tables(places):
    freq_steps = jnp.arange(32, dtype=jnp.float32)
    frequency = jnp.exp(freq_steps * (-2.0 / 64.0) * math.log(rope_base))
    angles = places.astype(jnp.float32)[:, None] * frequency[None, :]
    angles = jnp.concatenate([angles, angles], axis=1)
    return (jnp.cos(angles), jnp.sin(angles))


def rotate(values_in, cosine, sine_tab):
    half_width = values_in.shape[-1] // 2
    turned = jnp.concatenate([-values_in[..., half_width:], values_in[..., :half_width]], axis=-1)
    return values_in * cosine[:, None, :] + turned * sine_tab[:, None, :]


def unrotate(values_in, cosine, sine_tab):
    half_width = values_in.shape[-1] // 2
    scaled = values_in * sine_tab[:, None, :]
    turned_back = jnp.concatenate([scaled[..., half_width:], -scaled[..., :half_width]], axis=-1)
    return values_in * cosine[:, None, :] + turned_back


def layer_norm(values_in):
    average = jnp.mean(values_in, axis=-1, keepdims=True)
    centred = values_in - average
    spread = jnp.mean(centred * centred, axis=-1, keepdims=True)
    inv_scale = lax.rsqrt(spread + norm_eps)
    return (centred * inv_scale, inv_scale)


def norm_back(grad_h, normed, inv_scale, gain_row):
    grad_n = grad_h * gain_row
    return inv_scale * (
        grad_n
        - jnp.mean(grad_n, axis=-1, keepdims=True)
        - normed * jnp.mean(grad_n * normed, axis=-1, keepdims=True)
    )


def gelu_parts(gate_in):
    normal_cdf = 0.5 * (1.0 + lax.erf(gate_in * (1.0 / math.sqrt(2.0))))
    normal_pdf = jnp.exp(-0.5 * gate_in * gate_in) * (1.0 / math.sqrt(2.0 * math.pi))
    return (gate_in * normal_cdf, normal_cdf + gate_in * normal_pdf)


def contract_rows(left_side, right_side):
    return lax.dot_general(
        left_side, right_side, (((0,), (0,)), ((), ())), preferred_element_type=jnp.float32
    )


def contract_last(left_side, right_side):
    return lax.dot_general(
        left_side, right_side, (((1,), (1,)), ((), ())), preferred_element_type=jnp.float32
    )


def block_scores(block_query, head_keys, segment):
    scores = contract_last(block_query, head_keys) * score_scale
    allowed = segment[:, None] == segment[None, :]
    return jnp.where(allowed, scores, -1e30)


def attend(queries, key_rows, value_rows, segment, block_rows):
    head_outs = []
    head_sums = []
    for head_index in range(queries.shape[1] // 64):
        head_cols = slice(64 * head_index, 64 * head_index + 64)
        head_keys = key_rows[:, head_cols]
        head_values = value_rows[:, head_cols]
        block_query = queries[0:block_rows, head_cols]
        scores = block_scores(block_query, head_keys, segment)
        row_top = jnp.max(scores, axis=1, keepdims=True)
        logsum = row_top + jnp.log(jnp.sum(jnp.exp(scores - row_top), axis=1, keepdims=True))
        prob_block = jnp.exp(scores - logsum).astype(jnp.bfloat16)
        rows_out = jnp.dot(prob_block, head_values, preferred_element_type=jnp.float32).astype(
            jnp.bfloat16
        )
        rows_sum = logsum[:, 0]
        head_outs.append(rows_out)
        head_sums.append(rows_sum)
    return (jnp.concatenate(head_outs, axis=1), jnp.stack(head_sums))


def attend_back(queries, key_rows, value_rows, attended, grad_att, logsums, segment, block_rows):
    grads_q = []
    grads_k = []
    grads_v = []
    for head_index in range(queries.shape[1] // 64):
        head_cols = slice(64 * head_index, 64 * head_index + 64)
        head_query = queries[:, head_cols]
        head_keys = key_rows[:, head_cols]
        head_values = value_rows[:, head_cols]
        head_grad = grad_att[:, head_cols]
        row_delta = jnp.sum(
            head_grad.astype(jnp.float32) * attended[:, head_cols].astype(jnp.float32), axis=1
        )
        scores = block_scores(head_query, head_keys, segment)
        prob_full = jnp.exp(scores - logsums[head_index, 0:block_rows][:, None])
        grad_v = contract_rows(prob_full.astype(jnp.bfloat16), head_grad)
        grad_p = contract_last(head_grad, head_values)
        grad_s = (prob_full * (grad_p - row_delta[0:block_rows, None])).astype(jnp.bfloat16)
        query_blocks = jnp.dot(grad_s, head_keys, preferred_element_type=jnp.float32) * score_scale
        grad_k = contract_rows(grad_s, head_query) * score_scale
        grads_q.append(query_blocks)
        grads_k.append(grad_k)
        grads_v.append(grad_v)
    return (
        jnp.concatenate(grads_q, axis=1),
        jnp.concatenate(grads_k, axis=1),
        jnp.concatenate(grads_v, axis=1),
    )


def local(
    inputs,
    lengths,
    norm1_gain,
    qkv_weight,
    attn_out_weight,
    norm2_gain,
    ffn_in_weight,
    ffn_out_weight,
    out_grad,
):
    f32 = jnp.float32
    bf16 = jnp.bfloat16
    tok_dev = inputs.shape[0]
    model_width = inputs.shape[1]
    head_count = model_width // 64
    ctx_count = lax.axis_size("ctx")
    local_width = model_width // ctx_count
    local_heads = local_width // 64
    group_rows = tok_dev * ctx_count
    block_rows = 512
    shards = (norm1_gain, qkv_weight, attn_out_weight, norm2_gain, ffn_in_weight, ffn_out_weight)
    gain_one, w_qkv, w_attn, gain_two, w_in, w_out = (
        lax.all_gather(shards[0], ("fsdp", "ctx"), axis=0, tiled=True),
        lax.all_gather(shards[1], ("fsdp", "ctx"), axis=0, tiled=True),
        lax.all_gather(shards[2], ("fsdp", "ctx"), axis=0, tiled=True),
        lax.all_gather(shards[3], ("fsdp", "ctx"), axis=0, tiled=True),
        lax.all_gather(shards[4], ("fsdp", "ctx"), axis=0, tiled=True),
        lax.all_gather(shards[5], ("fsdp", "ctx"), axis=1, tiled=True),
    )
    index_rows = jnp.arange(group_rows, dtype=jnp.int32)
    segment, group_places = positions(lengths[0], index_rows)
    cos_group, sin_group = rope_tables(group_places)
    resid_in = inputs.astype(f32)
    normed_one, scale_one = layer_norm(resid_in)
    hidden_one = (normed_one * gain_one.astype(f32)).astype(bf16)
    local_places = lax.dynamic_slice_in_dim(group_places, lax.axis_index("ctx") * tok_dev, tok_dev)
    cos_local, sin_local = rope_tables(local_places)
    joined_out = jnp.dot(hidden_one, w_qkv, preferred_element_type=f32)
    queries = rotate(
        joined_out[:, :model_width].reshape(tok_dev, head_count, 64), cos_local, sin_local
    )
    queries = queries.reshape(tok_dev, model_width).astype(bf16)
    key_rows = rotate(
        joined_out[:, model_width : 2 * model_width].reshape(tok_dev, head_count, 64),
        cos_local,
        sin_local,
    )
    key_rows = key_rows.reshape(tok_dev, model_width).astype(bf16)
    value_rows = joined_out[:, 2 * model_width :].astype(bf16)
    query_heads, key_heads, value_heads = (
        lax.all_to_all(queries, "ctx", split_axis=1, concat_axis=0, tiled=True),
        lax.all_to_all(key_rows, "ctx", split_axis=1, concat_axis=0, tiled=True),
        lax.all_to_all(value_rows, "ctx", split_axis=1, concat_axis=0, tiled=True),
    )
    attended_heads, logsums = attend(query_heads, key_heads, value_heads, segment, block_rows)
    attended = lax.all_to_all(attended_heads, "ctx", split_axis=0, concat_axis=1, tiled=True)
    resid_mid = resid_in + jnp.dot(attended, w_attn, preferred_element_type=f32)
    normed_two, scale_two = layer_norm(resid_mid)
    hidden_two = (normed_two * gain_two.astype(f32)).astype(bf16)
    expanded = jnp.dot(hidden_two, w_in, preferred_element_type=f32)
    hidden_units = w_out.shape[0]
    gate_in = expanded[:, :hidden_units]
    up_in = expanded[:, hidden_units:]
    activated, gelu_slope = gelu_parts(gate_in)
    mixed_act = (activated * up_in).astype(bf16)
    outputs = (resid_mid + jnp.dot(mixed_act, w_out, preferred_element_type=f32)).astype(bf16)
    grad_mixed = contract_last(out_grad, w_out)
    grad_expanded = jnp.concatenate(
        [grad_mixed * up_in * gelu_slope, grad_mixed * activated], axis=1
    ).astype(bf16)
    grad_hidden_two = contract_last(grad_expanded, w_in)
    grad_gain_two = jnp.sum(grad_hidden_two * normed_two, axis=0)
    grad_mid = out_grad.astype(f32) + norm_back(
        grad_hidden_two, normed_two, scale_two, gain_two.astype(f32)
    )
    grad_mid_half = grad_mid.astype(bf16)
    grad_att = contract_last(grad_mid_half, w_attn).astype(bf16)
    grad_att_heads = lax.all_to_all(grad_att, "ctx", split_axis=1, concat_axis=0, tiled=True)
    grad_q_heads, grad_k_heads, grad_v_heads = attend_back(
        query_heads,
        key_heads,
        value_heads,
        attended_heads,
        grad_att_heads,
        logsums,
        segment,
        block_rows,
    )
    grad_q_heads = unrotate(grad_q_heads.reshape(group_rows, local_heads, 64), cos_group, sin_group)
    grad_q_heads = grad_q_heads.reshape(group_rows, local_width).astype(bf16)
    grad_k_heads = unrotate(grad_k_heads.reshape(group_rows, local_heads, 64), cos_group, sin_group)
    grad_k_heads = grad_k_heads.reshape(group_rows, local_width).astype(bf16)
    grad_v_heads = grad_v_heads.astype(bf16)
    grad_q, grad_k, grad_v = (
        lax.all_to_all(grad_q_heads, "ctx", split_axis=0, concat_axis=1, tiled=True),
        lax.all_to_all(grad_k_heads, "ctx", split_axis=0, concat_axis=1, tiled=True),
        lax.all_to_all(grad_v_heads, "ctx", split_axis=0, concat_axis=1, tiled=True),
    )
    grad_joined = jnp.concatenate([grad_q, grad_k, grad_v], axis=1)
    grad_hidden_one = contract_last(grad_joined, w_qkv)
    every_sum = lax.psum_scatter(
        jnp.concatenate(
            [
                contract_rows(hidden_one, grad_joined),
                jnp.concatenate(
                    [
                        contract_rows(attended, grad_mid_half),
                        contract_rows(hidden_two, grad_expanded),
                        contract_rows(out_grad, mixed_act),
                    ],
                    axis=1,
                ),
            ],
            axis=1,
        ),
        ("fsdp", "ctx"),
        scatter_dimension=0,
        tiled=True,
    )
    sum_w_qkv = every_sum[:, : 3 * model_width]
    rest_sums = every_sum[:, 3 * model_width :]
    grad_gain_one = jnp.sum(grad_hidden_one * normed_one, axis=0)
    input_grad = (
        grad_mid + norm_back(grad_hidden_one, normed_one, scale_one, gain_one.astype(f32))
    ).astype(bf16)
    sum_gain_one, sum_gain_two = (
        lax.psum_scatter(grad_gain_one, ("fsdp", "ctx"), scatter_dimension=0, tiled=True),
        lax.psum_scatter(grad_gain_two, ("fsdp", "ctx"), scatter_dimension=0, tiled=True),
    )
    sum_w_attn = rest_sums[:, :model_width]
    sum_w_in = rest_sums[:, model_width : model_width + 2 * hidden_units]
    sum_w_out = rest_sums[:, model_width + 2 * hidden_units :].T
    return (
        outputs,
        input_grad,
        sum_gain_one,
        sum_w_qkv,
        sum_w_attn,
        sum_gain_two,
        sum_w_in,
        sum_w_out,
    )


def solution(mesh):
    in_specs = (
        P(("fsdp", "ctx"), None),
        P("fsdp", None),
        P(("fsdp", "ctx")),
        P(("fsdp", "ctx"), None),
        P(("fsdp", "ctx"), None),
        P(("fsdp", "ctx")),
        P(("fsdp", "ctx"), None),
        P(None, ("fsdp", "ctx")),
        P(("fsdp", "ctx"), None),
    )
    out_specs = (
        P(("fsdp", "ctx"), None),
        P(("fsdp", "ctx"), None),
        P(("fsdp", "ctx")),
        P(("fsdp", "ctx"), None),
        P(("fsdp", "ctx"), None),
        P(("fsdp", "ctx")),
        P(("fsdp", "ctx"), None),
        P(None, ("fsdp", "ctx")),
    )
    return jax.shard_map(local, mesh=mesh, in_specs=in_specs, out_specs=out_specs, check_vma=False)
```

profile of v0, /device:TPU:0, one launch (start us, length us, event | category | flops | bytes accessed | tf_op | source)
XLA Modules:
  0.0 649.4 jit_solution(332151156606937224)
XLA Ops:
  11.9 42.2 %all-reduce.6 = (bf16[768]{0:T(1024)(128)(2,1)S(1)}, bf16[768]{0:T(1024)(128)(2,1)}) all-reduce(bf16[768]{0:T(1024)(128)(2,1)S(1)} %dynamic-update-slice, bf16[768]{0:T(1024)(128)(2,1)S(1)} %dynamic-update-slice.1), channel_id=1, replica_groups=mesh['fsdp'=8,'ctx'=4] {'fsdp','ctx'}, use_global_device_ids=true, to_apply=%add | all-reduce | flops 1536 | bytes 6144
  56.3 17.7 %all-gather.5.cloned.1.call-done = bf16[768,2304]{1,0:T(8,128)(2,1)} async-done(((bf16[24,2304]{1,0:T(8,128)(2,1)}), bf16[768,2304]{1,0:T(8,128)(2,1)}) %all-gather.5.cloned.1.call-update) | async-done | bytes 3538960 | tf_op jit(solution)/shard_map/all_gather | solution.py:160
  78.5 3.4 all-to-all-start
  84.1 3.2 all-to-all-done
  87.3 3.4 all-to-all-start.1
  90.7 5.2 all-to-all-done.1
  96.0 3.4 all-to-all-start.2
  101.2 3.7 all-to-all-done.2
  107.5 3.4 all-to-all-start.3
  114.6 14.8 %all-gather.7.cloned.1.call-done = bf16[768,768]{1,0:T(8,128)(2,1)} async-done(((bf16[24,768]{1,0:T(8,128)(2,1)}), bf16[768,768]{1,0:T(8,128)(2,1)}) %all-gather.7.cloned.1.call-update) | async-done | bytes 1179664 | tf_op jit(solution)/shard_map/all_gather | solution.py:161
  133.1 58.2 %all-gather.9.cloned.1.call-done = bf16[768,2304]{1,0:T(8,128)(2,1)} async-done(((bf16[24,2304]{1,0:T(8,128)(2,1)}), bf16[768,2304]{1,0:T(8,128)(2,1)}) %all-gather.9.cloned.1.call-update) | async-done | bytes 3538960 | tf_op jit(solution)/shard_map/all_gather | solution.py:163
  191.3 3.8 fusion.87
  195.0 53.2 %all-gather.11.cloned.1.call-done = bf16[1152,768]{0,1:T(8,128)(2,1)} async-done(((bf16[1152,24]{0,1:T(8,128)(2,1)}), bf16[1152,768]{0,1:T(8,128)(2,1)}) %all-gather.11.cloned.1.call-update) | async-done | bytes 1769488 | tf_op jit(solution)/shard_map/all_gather | solution.py:164
  258.5 4.2 all-to-all-start.4
  262.7 5.1 fusion.37
  280.3 3.4 all-to-all-start.7
  288.9 3.4 all-to-all-start.5
  297.6 4.0 all-to-all-start.6
  301.6 3.2 fusion.49
  311.2 7.4 %pad_maximum_fusion = f32[768,6528]{1,0:T(8,128)} fusion(f32[768,1152]{1,0:T(8,128)S(1)} %copy-done, f32[768,2304]{1,0:T(8,128)S(1)} %bitcast.116, f32[768,768]{1,0:T(8,128)S(1)} %copy-done.1, f32[768,2304]{1,0:T(8,128)S(1)} %fusion.39), kind=kLoop, calls=%fused_computation | loop fusion | flops 15040512 | bytes 40108032 | tf_op jit(solution)/shard_map/concatenate | solution.py:238
  319.9 2.8 fusion.6
  322.7 4.3 fusion.31
  327.1 39.3 %all-reduce.5 = (f32[768]{0:T(1024)S(1)}, f32[768]{0:T(1024)S(1)}) all-reduce(f32[768]{0:T(1024)S(1)} %get-tuple-element.10, f32[768]{0:T(1024)S(1)} %copy-done.41), channel_id=2, replica_groups=mesh['fsdp'=8,'ctx'=4] {'fsdp','ctx'}, use_global_device_ids=true, to_apply=%region_21.22.clone | all-reduce | flops 1536 | bytes 12288
  369.4 268.4 %all-reduce.9.cloned.1.call-done = f32[768,6528]{1,0:T(8,128)} async-done(((f32[768,6528]{1,0:T(8,128)}), f32[768,6528]{1,0:T(8,128)}) %all-reduce.9.cloned.1.call-update) | async-done | bytes 20054032
  (221 shorter events, 73.8 us)
Async XLA Ops:
  7.2 48.8 %copy-start.2 = (bf16[128,768]{1,0:T(8,128)(2,1)S(1)}, bf16[128,768]{1,0:T(8,128)(2,1)}, u32[]{:S(2)}) copy-start(bf16[128,768]{1,0:T(8,128)(2,1)} %param.9) | copy-start | bytes 589828
  7.2 66.8 %all-gather.5.cloned.1.call-start = ((), (), s32[]{:S(2)}) async-start(), calls=%async_computation.8 | async-start | bytes 3649536 | tf_op jit(solution)/shard_map/all_gather | solution.py:160
  7.9 121.5 %all-gather.7.cloned.1.call-start = ((), (), s32[]{:S(2)}) async-start(), calls=%async_computation.9 | async-start | bytes 1216512 | tf_op jit(solution)/shard_map/all_gather | solution.py:161
  8.7 182.6 %all-gather.9.cloned.1.call-start = ((), (), s32[]{:S(2)}) async-start(), calls=%async_computation.10 | async-start | bytes 3649536 | tf_op jit(solution)/shard_map/all_gather | solution.py:163
  54.1 22.5 %copy-start.42 = (f32[32]{0:T(128)}, f32[32]{0:T(128)S(1)}, u32[]{:S(2)}) copy-start(f32[32]{0:T(128)S(1)} %multiply_exponential_fusion) | copy-start | bytes 388
  56.1 20.6 %copy-start.33 = (f32[128]{0:T(128)}, f32[128]{0:T(128)S(1)}, u32[]{:S(2)}) copy-start(f32[128]{0:T(128)S(1)} %broadcast_multiply_fusion.9) | copy-start | bytes 1540
  56.3 20.4 %copy-start.37 = (f32[128]{0:T(128)}, f32[128]{0:T(128)S(1)}, u32[]{:S(2)}) copy-start(f32[128]{0:T(128)S(1)} %add_rsqrt_fusion.1) | copy-start | bytes 1540
  78.5 8.8 %all-to-all-start = ((bf16[128,4,192]{0,2,1:T(8,128)(2,1)}), bf16[128,4,192]{0,2,1:T(8,128)(2,1)S(1)}, u32[]{:S(2)}, u32[]{:S(2)}) async-start(bf16[128,4,192]{0,2,1:T(8,128)(2,1)} %bitcast.7), calls=%async_computation | async-start | bytes 393216 | tf_op jit(solution)/shard_map/all_to_all | solution.py:187
  81.9 166.4 %all-gather.11.cloned.1.call-start = ((), (), s32[]{:S(2)}) async-start(), calls=%async_computation.11 | async-start | bytes 1824768 | tf_op jit(solution)/shard_map/all_gather | solution.py:164
  87.3 8.6 %all-to-all-start.1 = ((bf16[128,4,192]{0,2,1:T(8,128)(2,1)}), bf16[128,4,192]{0,2,1:T(8,128)(2,1)S(1)}, u32[]{:S(2)}, u32[]{:S(2)}) async-start(bf16[128,4,192]{0,2,1:T(8,128)(2,1)} %bitcast.11), calls=%async_computation.1 | async-start | bytes 393216 | tf_op jit(solution)/shard_map/all_to_all | solution.py:188
  90.7 9.4 %copy-start.14 = (bf16[512,192]{0,1:T(8,128)(2,1)}, bf16[512,192]{0,1:T(8,128)(2,1)S(1)}, u32[]{:S(2)}) copy-start(bf16[512,192]{0,1:T(8,128)(2,1)S(1)} %copy_bitcast_fusion.2) | copy-start | bytes 589828
  96.0 8.9 %all-to-all-start.2 = ((bf16[128,4,192]{0,2,1:T(8,128)(2,1)}), bf16[128,4,192]{0,2,1:T(8,128)(2,1)S(1)}, u32[]{:S(2)}, u32[]{:S(2)}) async-start(bf16[128,4,192]{0,2,1:T(8,128)(2,1)} %bitcast.13), calls=%async_computation.2 | async-start | bytes 393216 | tf_op jit(solution)/shard_map/all_to_all | solution.py:189
  107.5 21.9 %all-to-all-start.3 = ((bf16[4,128,192]{1,2,0:T(8,128)(2,1)}), bf16[4,128,192]{1,2,0:T(8,128)(2,1)S(1)}, u32[]{:S(2)}, u32[]{:S(2)}) async-start(bf16[4,128,192]{1,2,0:T(8,128)(2,1)} %copy_bitcast_fusion.4), calls=%async_computation.3 | async-start | bytes 393216 | tf_op jit(solution)/shard_map/all_to_all | solution.py:192
  258.5 9.4 %all-to-all-start.4 = ((bf16[128,4,192]{0,2,1:T(8,128)(2,1)}), bf16[128,4,192]{0,2,1:T(8,128)(2,1)}, u32[]{:S(2)}, u32[]{:S(2)}) async-start(bf16[128,4,192]{0,2,1:T(8,128)(2,1)} %bitcast.126), calls=%async_computation.4 | async-start | bytes 393216 | tf_op jit(solution)/shard_map/all_to_all | solution.py:214
  280.3 8.6 %all-to-all-start.7 = ((bf16[4,128,192]{1,2,0:T(8,128)(2,1)}), bf16[4,128,192]{1,2,0:T(8,128)(2,1)S(1)}, u32[]{:S(2)}, u32[]{:S(2)}) async-start(bf16[4,128,192]{1,2,0:T(8,128)(2,1)} %pad_maximum_fusion.11), calls=%async_computation.7 | async-start | bytes 393216 | tf_op jit(solution)/shard_map/all_to_all | solution.py:233
  284.8 7.5 %copy-start.5 = (f32[128,2304]{1,0:T(8,128)S(1)}, f32[128,2304]{1,0:T(8,128)}, u32[]{:S(2)}) copy-start(f32[128,2304]{1,0:T(8,128)} %fusion.87) | copy-start | bytes 3538948
  284.8 7.5 %copy-start.13 = (bf16[128,768]{1,0:T(8,128)(2,1)S(1)}, bf16[128,768]{1,0:T(8,128)(2,1)}, u32[]{:S(2)}) copy-start(bf16[128,768]{1,0:T(8,128)(2,1)} %param.17) | copy-start | bytes 589828
  288.9 8.6 %all-to-all-start.5 = ((bf16[4,128,192]{1,2,0:T(8,128)(2,1)}), bf16[4,128,192]{1,2,0:T(8,128)(2,1)S(1)}, u32[]{:S(2)}, u32[]{:S(2)}) async-start(bf16[4,128,192]{1,2,0:T(8,128)(2,1)} %copy.121), calls=%async_computation.5 | async-start | bytes 393216 | tf_op jit(solution)/shard_map/all_to_all | solution.py:231
  295.5 11.4 %copy-start.3 = (bf16[128,768]{1,0:T(8,128)(2,1)S(1)}, bf16[128,768]{1,0:T(8,128)(2,1)}, u32[]{:S(2)}) copy-start(bf16[128,768]{1,0:T(8,128)(2,1)} %param.9) | copy-start | bytes 589828
  295.6 11.4 %copy-start.34 = (f32[128]{0:T(128)S(1)}, f32[128]{0:T(128)}, u32[]{:S(2)}) copy-start(f32[128]{0:T(128)} %copy-done.33) | copy-start | bytes 1540
  295.6 11.4 %copy-start.38 = (f32[128]{0:T(128)S(1)}, f32[128]{0:T(128)}, u32[]{:S(2)}) copy-start(f32[128]{0:T(128)} %copy-done.37) | copy-start | bytes 1540
  297.6 9.4 %all-to-all-start.6 = ((bf16[4,128,192]{1,2,0:T(8,128)(2,1)}), bf16[4,128,192]{1,2,0:T(8,128)(2,1)}, u32[]{:S(2)}, u32[]{:S(2)}) async-start(bf16[4,128,192]{1,2,0:T(8,128)(2,1)} %copy.122), calls=%async_computation.6 | async-start | bytes 393216 | tf_op jit(solution)/shard_map/all_to_all | solution.py:232
  301.6 336.2 %all-reduce.9.cloned.1.call-start = ((), (), s32[]{:S(2)}) async-start(), calls=%async_computation.12 | async-start | bytes 40108032
  301.6 7.8 %slice-start = ((s8[7077888]{0:T(1024)(128)(4,1)}), s8[2883584]{0:T(1024)(128)(4,1)S(1)}, s32[]{:S(2)}) async-start(s8[7077888]{0:T(1024)(128)(4,1)} %bitcast.115), calls=%async_computation.13 | async-start | bytes 5767168
  (36 other events, 109.5 us)
Sparse Core Ops, SparseCore 0:
  10.9 63.0 all-gather.4
  76.8 52.5 all-gather.6
  132.3 58.9 all-gather.8
  194.0 54.2 all-gather.10
  318.8 318.9 all-reduce.8
where the time goes:
time: 651 us; the launch traced here: 649 us
  waiting for transfers between devices  433 us (67%)
  blocking collectives  81.5 us (13%)
  matrix products  42.7 us (7%)
  local copies, waits for them, and re-layouts  29.3 us (5%)
  starting transfers between devices  28.6 us (4%)
  other arithmetic  19.8 us (3%)
  between operations  14.6 us (2%)
    unnamed x6, waiting for transfers between devices  271 us
    unnamed x2, blocking collectives  81.5 us
    all_gather x1, waiting for transfers between devices, local(): lax.all_gather(shards[4], ('fsdp', 'ctx'), axis=0, tiled=True)  58.2 us
    all_gather x1, waiting for transfers between devices, local(): lax.all_gather(shards[5], ('fsdp', 'ctx'), axis=1, tiled=True)  53.2 us
    all_gather x1, waiting for transfers between devices, local(): lax.all_gather(shards[1], ('fsdp', 'ctx'), axis=0, tiled=True)  17.7 us
    dot_general x10, matrix products, contract_rows(): lax.dot_general(left_side, right_side, (((0,), (0,)), ((), ())), preferre...  17 us
    all_gather x1, waiting for transfers between devices, local(): lax.all_gather(shards[2], ('fsdp', 'ctx'), axis=0, tiled=True)  14.8 us
    dot_general x10, matrix products, contract_last(): lax.dot_general(left_side, right_side, (((1,), (1,)), ((), ())), preferre...  13.2 us
  transfers between devices with their start and end apart: 13, of which 11 were waited for; matrix products, arithmetic and copies ran while one was open for 7% of the time, Pallas kernels for 0%

commit v1 on v0

--- a/solution.py
+++ b/solution.py
@@ -7,6 +7,28 @@
 rope_base = 160000.0
 norm_eps = 1e-05
 score_scale = 0.125
+
+
+def joined_along(pieces, dim):
+    pieces = jnp.moveaxis(pieces, 0, dim)
+    dims = pieces.shape
+    return pieces.reshape(*dims[:dim], dims[dim] * dims[dim + 1], *dims[dim + 2 :])
+
+
+def doubled(shard, axis):
+    size = lax.axis_size(axis)
+    tiles = shard[None]
+    for level in range(size.bit_length() - 1):
+        bit = 1 << level
+        other = lax.ppermute(tiles, axis, [(i, i ^ bit) for i in range(size)])
+        both = jnp.stack([tiles, other])
+        upper = lax.axis_index(axis) >> level & 1
+        tiles = jnp.where(upper == 0, both, both[::-1]).reshape(-1, *shard.shape)
+    return tiles
+
+
+def doubled_up(x, axis, dim):
+    return joined_along(doubled(x, axis), dim)
 
 
 def positions(length_row, index_rows):
@@ -161,7 +183,7 @@
         lax.all_gather(shards[2], ("fsdp", "ctx"), axis=0, tiled=True),
         lax.all_gather(shards[3], ("fsdp", "ctx"), axis=0, tiled=True),
         lax.all_gather(shards[4], ("fsdp", "ctx"), axis=0, tiled=True),
-        lax.all_gather(shards[5], ("fsdp", "ctx"), axis=1, tiled=True),
+        doubled_up(shards[5], ("fsdp", "ctx"), 1),
     )
     index_rows = jnp.arange(group_rows, dtype=jnp.int32)
     segment, group_places = positions(lengths[0], index_rows)

time: 651 us -> 616 us (0.946)
  waiting for transfers between devices: 433 us -> 380 us
  starting transfers between devices: 28.6 us -> 36.5 us
  other arithmetic: 19.8 us -> 27.4 us
    all_gather x1 -> x0, waiting for transfers between devices: 53.2 us -> none  [local(): lax.all_gather(shards[5], ('fsdp', 'ctx'), axis=1, tiled=True)]
    ppermute x0 -> x5, waiting for transfers between devices: none -> 45.7 us  [doubled(): other = lax.ppermute(tiles, axis, [(i, i ^ bit) for i in range(size)])]
    all_gather x1, waiting for transfers between devices: 17.7 us -> 0.01 us  [local(): lax.all_gather(shards[1], ('fsdp', 'ctx'), axis=0, tiled=True)]
    all_gather x1, waiting for transfers between devices: 14.8 us -> 0.01 us  [local(): lax.all_gather(shards[2], ('fsdp', 'ctx'), axis=0, tiled=True)]
    all_gather x1, waiting for transfers between devices: 58.2 us -> 48.7 us  [local(): lax.all_gather(shards[4], ('fsdp', 'ctx'), axis=0, tiled=True)]
    ppermute x0 -> x5, starting transfers between devices: none -> 7.46 us  [doubled(): other = lax.ppermute(tiles, axis, [(i, i ^ bit) for i in range(size)])]
    unnamed x6 -> x5, waiting for transfers between devices: 271 us -> 269 us
  transfers between devices with their start and end apart: 13 -> 17, of which waited for: 11 -> 12; matrix products, arithmetic and copies ran while one was open for 7% -> 9% of each run, Pallas kernels for 0% -> 0%
where the time goes in v1:
time: 616 us; the launch traced here: 614 us
  waiting for transfers between devices  380 us (62%)
  blocking collectives  82.7 us (13%)
  matrix products  39.6 us (6%)
  starting transfers between devices  36.5 us (6%)
  local copies, waits for them, and re-layouts  33 us (5%)
  other arithmetic  27.4 us (4%)
  between operations  14.6 us (2%)
    unnamed x5, waiting for transfers between devices  269 us
    unnamed x2, blocking collectives  82.7 us
    all_gather x1, waiting for transfers between devices, local(): lax.all_gather(shards[4], ('fsdp', 'ctx'), axis=0, tiled=True)  48.7 us
    ppermute x5, waiting for transfers between devices, doubled(): other = lax.ppermute(tiles, axis, [(i, i ^ bit) for i in range(size)])  45.7 us
    dot_general x10, matrix products, contract_rows(): lax.dot_general(left_side, right_side, (((0,), (0,)), ((), ())), preferre...  17 us
  transfers between devices with their start and end apart: 17, of which 12 were waited for; matrix products, arithmetic and copies ran while one was open for 9% of the time, Pallas kernels for 0%

profile of v1, /device:TPU:0, one launch (start us, length us, event | category | flops | bytes accessed | tf_op | source)
XLA Modules:
  0.0 613.9 jit_solution(12159003029157022318)
XLA Ops:
  13.9 42.4 %all-reduce.6 = (bf16[768]{0:T(1024)(128)(2,1)S(1)}, bf16[768]{0:T(1024)(128)(2,1)S(1)}) all-reduce(bf16[768]{0:T(1024)(128)(2,1)S(1)} %dynamic-update-slice, bf16[768]{0:T(1024)(128)(2,1)S(1)} %dynamic-update-slice.1), channel_id=1, replica_groups=mesh['fsdp'=8,'ctx'=4] {'fsdp','ctx'}, use_global_device_ids=true, to_apply=%add | all-reduce | flops 1536 | bytes 6144
  59.7 5.4 collective-permute-done.1
  67.1 4.1 collective-permute-done.2
  73.0 9.6 %collective-permute-done.3 = bf16[8,1152,24]{1,2,0:T(8,128)(2,1)S(1)} collective-permute-done((bf16[8,1152,24]{1,2,0:T(8,128)(2,1)S(1)}, bf16[8,1152,24]{1,2,0:T(8,128)(2,1)S(1)}, u32[]{:S(2)}, u32[]{:S(2)}) %collective-permute-start.3) | collective-permute-done | bytes 442400 | tf_op jit(solution)/shard_map/ppermute | solution.py:23
  93.9 3.9 all-to-all-start
  97.8 26.7 %collective-permute-done.4 = bf16[16,1152,24]{1,2,0:T(8,128)(2,1)} collective-permute-done((bf16[16,1152,24]{1,2,0:T(8,128)(2,1)S(1)}, bf16[16,1152,24]{1,2,0:T(8,128)(2,1)}, u32[]{:S(2)}, u32[]{:S(2)}) %collective-permute-start.4) | collective-permute-done | bytes 884768 | tf_op jit(solution)/shard_map/ppermute | solution.py:23
  128.7 3.4 all-to-all-start.1
  132.1 5.8 all-to-all-done.1
  138.0 3.4 all-to-all-start.2
  143.1 3.5 all-to-all-done.2
  149.2 3.4 all-to-all-start.3
  152.6 3.6 reverse_select_fusion
  161.6 48.7 %all-gather.8.cloned.1.call-done = bf16[768,2304]{1,0:T(8,128)(2,1)} async-done(((bf16[24,2304]{1,0:T(8,128)(2,1)}), bf16[768,2304]{1,0:T(8,128)(2,1)}) %all-gather.8.cloned.1.call-update) | async-done | bytes 3538960 | tf_op jit(solution)/shard_map/all_gather | solution.py:185
  210.3 2.9 fusion.89
  223.1 4.2 all-to-all-start.4
  227.3 5.1 fusion.37
  244.9 3.4 all-to-all-start.7
  253.6 3.4 all-to-all-start.5
  262.2 4.0 all-to-all-start.6
  266.3 3.2 fusion.49
  275.8 7.4 %pad_maximum_fusion = f32[768,6528]{1,0:T(8,128)} fusion(f32[768,1152]{1,0:T(8,128)S(1)} %copy-done, f32[768,2304]{1,0:T(8,128)S(1)} %bitcast.140, f32[768,768]{1,0:T(8,128)S(1)} %copy-done.1, f32[768,2304]{1,0:T(8,128)S(1)} %fusion.39), kind=kLoop, calls=%fused_computation | loop fusion | flops 15040512 | bytes 40108032 | tf_op jit(solution)/shard_map/concatenate | solution.py:260
  287.3 4.2 fusion.31
  291.6 40.3 %all-reduce.5 = (f32[768]{0:T(1024)S(1)}, f32[768]{0:T(1024)S(1)}) all-reduce(f32[768]{0:T(1024)S(1)} %get-tuple-element.10, f32[768]{0:T(1024)S(1)} %copy-done.43), channel_id=2, replica_groups=mesh['fsdp'=8,'ctx'=4] {'fsdp','ctx'}, use_global_device_ids=true, to_apply=%region_21.22.clone | all-reduce | flops 1536 | bytes 12288
  334.9 267.4 %all-reduce.9.cloned.1.call-done = f32[768,6528]{1,0:T(8,128)} async-done(((f32[768,6528]{1,0:T(8,128)}), f32[768,6528]{1,0:T(8,128)}) %all-reduce.9.cloned.1.call-update) | async-done | bytes 20054032
  (236 shorter events, 90.2 us)
Async XLA Ops:
  7.2 50.0 %copy-start.33 = (bf16[1152,24]{0,1:T(8,128)(2,1)S(1)}, bf16[1152,24]{0,1:T(8,128)(2,1)}, u32[]{:S(2)}) copy-start(bf16[1152,24]{0,1:T(8,128)(2,1)} %param.16) | copy-start | bytes 165892
  7.2 52.4 %copy-start.2 = (bf16[128,768]{1,0:T(8,128)(2,1)S(1)}, bf16[128,768]{1,0:T(8,128)(2,1)}, u32[]{:S(2)}) copy-start(bf16[128,768]{1,0:T(8,128)(2,1)} %param.9) | copy-start | bytes 589828
  7.2 77.1 %all-gather.4.cloned.1.call-start = ((), (), s32[]{:S(2)}) async-start(), calls=%async_computation.8 | async-start | bytes 3649536 | tf_op jit(solution)/shard_map/all_gather | solution.py:182
  7.9 148.3 %all-gather.6.cloned.1.call-start = ((), (), s32[]{:S(2)}) async-start(), calls=%async_computation.9 | async-start | bytes 1216512 | tf_op jit(solution)/shard_map/all_gather | solution.py:183
  8.7 201.7 %all-gather.8.cloned.1.call-start = ((), (), s32[]{:S(2)}) async-start(), calls=%async_computation.10 | async-start | bytes 3649536 | tf_op jit(solution)/shard_map/all_gather | solution.py:185
  8.7 48.5 %collective-permute-start = (bf16[1,1152,24]{1,2,0:T(8,128)(2,1)}, bf16[1,1152,24]{1,2,0:T(8,128)(2,1)S(1)}, u32[]{:S(2)}, u32[]{:S(2)}) collective-permute-start(bf16[1,1152,24]{1,2,0:T(8,128)(2,1)} %bitcast.169), channel_id=1, source_target_pairs={{0,1},{1,0},{2,3},{3,2},{4,5},{5,4},{6,7},{7,6},{8,9},{9,8},{10,11... | collective-permute-start | bytes 165896 | tf_op jit(solution)/shard_map/ppermute | solution.py:23
  57.3 7.8 %collective-permute-start.1 = (bf16[2,1152,24]{1,2,0:T(8,128)(2,1)S(1)}, bf16[2,1152,24]{1,2,0:T(8,128)(2,1)S(1)}, u32[]{:S(2)}, u32[]{:S(2)}) collective-permute-start(bf16[2,1152,24]{1,2,0:T(8,128)(2,1)S(1)} %get-tuple-element.42), channel_id=1, source_target_pairs={{0,2},{1,3},{2,0},{3,1},{4,6},{5,7},{6,4},{7,5},{8,10},{9,11},{10,... | collective-permute-start | bytes 331784 | tf_op jit(solution)/shard_map/ppermute | solution.py:23
  65.2 6.0 collective-permute-start.2
  67.1 17.2 %copy-start.36 = (f32[128]{0:T(128)}, f32[128]{0:T(128)S(1)}, u32[]{:S(2)}) copy-start(f32[128]{0:T(128)S(1)} %broadcast_multiply_fusion.9) | copy-start | bytes 1540
  71.3 11.3 %collective-permute-start.3 = (bf16[8,1152,24]{1,2,0:T(8,128)(2,1)S(1)}, bf16[8,1152,24]{1,2,0:T(8,128)(2,1)S(1)}, u32[]{:S(2)}, u32[]{:S(2)}) collective-permute-start(bf16[8,1152,24]{1,2,0:T(8,128)(2,1)S(1)} %bitcast.145), channel_id=1, source_target_pairs={{0,8},{1,9},{2,10},{3,11},{4,12},{5,13},{6,14},{7,15},{8,0},{9,1},... | collective-permute-start | bytes 1327112 | tf_op jit(solution)/shard_map/ppermute | solution.py:23
  73.0 11.2 %copy-start.40 = (f32[128]{0:T(128)}, f32[128]{0:T(128)S(1)}, u32[]{:S(2)}) copy-start(f32[128]{0:T(128)S(1)} %add_rsqrt_fusion.1) | copy-start | bytes 1540
  82.8 41.6 %collective-permute-start.4 = (bf16[16,1152,24]{1,2,0:T(8,128)(2,1)S(1)}, bf16[16,1152,24]{1,2,0:T(8,128)(2,1)}, u32[]{:S(2)}, u32[]{:S(2)}) collective-permute-start(bf16[16,1152,24]{1,2,0:T(8,128)(2,1)S(1)} %bitcast.143), channel_id=1, source_target_pairs={{0,16},{1,17},{2,18},{3,19},{4,20},{5,21},{6,22},{7,23},{8,24},{9,... | collective-permute-start | bytes 2654216 | tf_op jit(solution)/shard_map/ppermute | solution.py:23
  93.9 34.9 %all-to-all-start = ((bf16[128,4,192]{0,2,1:T(8,128)(2,1)}), bf16[128,4,192]{0,2,1:T(8,128)(2,1)S(1)}, u32[]{:S(2)}, u32[]{:S(2)}) async-start(bf16[128,4,192]{0,2,1:T(8,128)(2,1)} %bitcast.7), calls=%async_computation | async-start | bytes 393216 | tf_op jit(solution)/shard_map/all_to_all | solution.py:209
  128.7 9.2 %all-to-all-start.1 = ((bf16[128,4,192]{0,2,1:T(8,128)(2,1)}), bf16[128,4,192]{0,2,1:T(8,128)(2,1)S(1)}, u32[]{:S(2)}, u32[]{:S(2)}) async-start(bf16[128,4,192]{0,2,1:T(8,128)(2,1)} %bitcast.11), calls=%async_computation.1 | async-start | bytes 393216 | tf_op jit(solution)/shard_map/all_to_all | solution.py:210
  138.0 8.6 %all-to-all-start.2 = ((bf16[128,4,192]{0,2,1:T(8,128)(2,1)}), bf16[128,4,192]{0,2,1:T(8,128)(2,1)S(1)}, u32[]{:S(2)}, u32[]{:S(2)}) async-start(bf16[128,4,192]{0,2,1:T(8,128)(2,1)} %bitcast.13), calls=%async_computation.2 | async-start | bytes 393216 | tf_op jit(solution)/shard_map/all_to_all | solution.py:211
  149.2 8.6 %all-to-all-start.3 = ((bf16[4,128,192]{1,2,0:T(8,128)(2,1)}), bf16[4,128,192]{1,2,0:T(8,128)(2,1)S(1)}, u32[]{:S(2)}, u32[]{:S(2)}) async-start(bf16[4,128,192]{1,2,0:T(8,128)(2,1)} %copy_bitcast_fusion.4), calls=%async_computation.3 | async-start | bytes 393216 | tf_op jit(solution)/shard_map/all_to_all | solution.py:214
  223.1 9.4 %all-to-all-start.4 = ((bf16[128,4,192]{0,2,1:T(8,128)(2,1)}), bf16[128,4,192]{0,2,1:T(8,128)(2,1)}, u32[]{:S(2)}, u32[]{:S(2)}) async-start(bf16[128,4,192]{0,2,1:T(8,128)(2,1)} %bitcast.158), calls=%async_computation.4 | async-start | bytes 393216 | tf_op jit(solution)/shard_map/all_to_all | solution.py:236
  244.9 8.6 %all-to-all-start.7 = ((bf16[4,128,192]{1,2,0:T(8,128)(2,1)}), bf16[4,128,192]{1,2,0:T(8,128)(2,1)S(1)}, u32[]{:S(2)}, u32[]{:S(2)}) async-start(bf16[4,128,192]{1,2,0:T(8,128)(2,1)} %pad_maximum_fusion.15), calls=%async_computation.7 | async-start | bytes 393216 | tf_op jit(solution)/shard_map/all_to_all | solution.py:255
  253.6 8.6 %all-to-all-start.5 = ((bf16[4,128,192]{1,2,0:T(8,128)(2,1)}), bf16[4,128,192]{1,2,0:T(8,128)(2,1)S(1)}, u32[]{:S(2)}, u32[]{:S(2)}) async-start(bf16[4,128,192]{1,2,0:T(8,128)(2,1)} %copy.126), calls=%async_computation.5 | async-start | bytes 393216 | tf_op jit(solution)/shard_map/all_to_all | solution.py:253
  260.2 11.4 %copy-start.3 = (bf16[128,768]{1,0:T(8,128)(2,1)S(1)}, bf16[128,768]{1,0:T(8,128)(2,1)}, u32[]{:S(2)}) copy-start(bf16[128,768]{1,0:T(8,128)(2,1)} %param.9) | copy-start | bytes 589828
  260.2 11.4 %copy-start.37 = (f32[128]{0:T(128)S(1)}, f32[128]{0:T(128)}, u32[]{:S(2)}) copy-start(f32[128]{0:T(128)} %copy-done.36) | copy-start | bytes 1540
  260.2 11.4 %copy-start.41 = (f32[128]{0:T(128)S(1)}, f32[128]{0:T(128)}, u32[]{:S(2)}) copy-start(f32[128]{0:T(128)} %copy-done.40) | copy-start | bytes 1540
  262.2 9.4 %all-to-all-start.6 = ((bf16[4,128,192]{1,2,0:T(8,128)(2,1)}), bf16[4,128,192]{1,2,0:T(8,128)(2,1)}, u32[]{:S(2)}, u32[]{:S(2)}) async-start(bf16[4,128,192]{1,2,0:T(8,128)(2,1)} %copy.127), calls=%async_computation.6 | async-start | bytes 393216 | tf_op jit(solution)/shard_map/all_to_all | solution.py:254
  266.2 336.1 %all-reduce.9.cloned.1.call-start = ((), (), s32[]{:S(2)}) async-start(), calls=%async_computation.11 | async-start | bytes 40108032
  (39 other events, 131.6 us)
Sparse Core Ops, SparseCore 0:
  10.9 64.5 all-gather.3
  78.4 70.0 all-gather.5
  151.4 58.8 all-gather.7
  283.4 318.8 all-reduce.8
